TPU v7x, 32 devices: a whole 2x2x4 slice. The times are simulated.
32 devices in a mesh: groups: 2 (over y), date: 4 (over z), rng: 2 (over x), az: 2 (over core).
Axes of the slice: x: 2, y: 2, z: 4, core: 2. Of those that a mesh axis runs over, the one named last changes fastest.
Arguments:
- slc: bfloat16 [2, 8, 64, 5120], P(None, ('groups', 'date'), 'az', 'rng'), parts along dimension 1, may hold values from -24 to 24
- offsets: int32 [8, 2], P(('groups', 'date')), parts along dimension 0, may hold values from -24 to 24, as said below
- kernel_index: int32 [8, 2], P(('groups', 'date')), parts along dimension 0, may hold values from 0 to 15
- range_shift: float32 [8], P('groups'), parts along dimension 0, may hold values from -0.15 to 0.15
Outputs:
- ifg: float32 [2, 8, 8, 16, 256], P(None, ('groups', 'date'), None, 'az', 'rng'), parts along dimension 1
There are 2 independent parts, one for each index of `groups`. A program takes and returns all parts, laid end to end along the dimension named above; each array names one. Nothing has to cross between parts.
Inputs may be any that keep to these rules, and one draw needn't show every extreme that they name: `offsets`: column 0 is the azimuth offset, within -8 to 8; column 1 is the range offset. Both ends of both ranges are taken by some date.
All inputs are finite; a program needn't handle non-finite values.
Results may differ from a plain program's by a relative error of at most 0.0039.
Values may be sent and summed in bfloat16 or wider, within the bound.
A program may use at most 64 MiB of HBM per device.

v0:
```python
import jax
import jax.numpy as jnp
from jax import lax
from jax.sharding import PartitionSpec as P

LAGS = 8
KERNELS = 16
FILTER_HALF = 8
LOOK_AZ = 4
LOOK_RG = 20
HALO_AZ = 12
HALO_RG = 36


def padded(cells, sides, width):
    for axis, dim in sides:
        count = lax.axis_size(axis)
        ends = count - 1
        head = lax.slice_in_dim(cells, 0, width, axis=dim)
        tail = lax.slice_in_dim(cells, cells.shape[dim] - width, cells.shape[dim], axis=dim)
        cells = jnp.concatenate(
            [
                lax.ppermute(tail, axis, [(i, (i + 1) % count) for i in range(ends)]),
                cells,
                lax.ppermute(head, axis, [((i + 1) % count, i) for i in range(ends)]),
            ],
            axis=dim,
        )
    return cells


def shifted(value, axis, steps):
    count = lax.axis_size(axis)
    leading, last = (max(0, -steps), min(count, count - steps))
    return lax.ppermute(value, axis, [(source, source + steps) for source in range(leading, last)])


def kernel_taps(index):
    fraction = index.astype(jnp.float32) / KERNELS
    position = jnp.arange(8, dtype=jnp.float32) - 3.0 - fraction
    shaped = jnp.sinc(position) * (0.5 + 0.5 * jnp.cos(jnp.pi * position / 5.0))
    return shaped / jnp.sum(shaped)


def lowpass_taps(band_gap):
    spacing = jnp.arange(2 * FILTER_HALF + 1, dtype=jnp.float32) - FILTER_HALF
    window = (
        0.4
        * jnp.sinc(0.4 * spacing)
        * (0.54 + 0.46 * jnp.cos(jnp.pi * spacing / (FILTER_HALF + 1)))
    )
    phase_angle = jnp.pi * band_gap * spacing
    return (window * jnp.cos(phase_angle), window * jnp.sin(phase_angle))


def resample(source, shift_pair, kernel_pair, line_count, column_count):
    span_width = column_count + 2 * FILTER_HALF
    line_start = HALO_AZ + shift_pair[0] - 3
    column_start = HALO_RG - FILTER_HALF + shift_pair[1] - 3
    window = lax.dynamic_slice(
        source, (jnp.int32(0), line_start, column_start), (2, line_count + 7, span_width + 7)
    ).astype(jnp.float32)
    column_taps = kernel_taps(kernel_pair[1])
    line_taps = kernel_taps(kernel_pair[0])
    across = sum((column_taps[q] * window[:, :, q : q + span_width] for q in range(8)))
    return sum((line_taps[p] * across[:, p : p + line_count, :] for p in range(8))).astype(
        jnp.bfloat16
    )


def spectral_gap(range_shift, own_date, other_date):
    own_value = lax.dynamic_index_in_dim(range_shift, own_date, 0, keepdims=False)
    other_value = lax.dynamic_index_in_dim(range_shift, other_date, 0, keepdims=False)
    return own_value - other_value


def pair_looks(master, partner, band_gap):
    cos_taps, sin_taps = lowpass_taps(band_gap)
    column_count = master.shape[-1] - 2 * FILTER_HALF
    line_count = master.shape[1]
    master_re = jnp.zeros((line_count, column_count), jnp.float32)
    master_im = master_re
    partner_re = master_re
    partner_im = master_re
    for t in range(2 * FILTER_HALF + 1):
        first_part = master[:, :, t : t + column_count].astype(jnp.float32)
        second_part = partner[:, :, t : t + column_count].astype(jnp.float32)
        master_re = master_re + cos_taps[t] * first_part[0] + sin_taps[t] * first_part[1]
        master_im = master_im + cos_taps[t] * first_part[1] - sin_taps[t] * first_part[0]
        partner_re = partner_re + cos_taps[t] * second_part[0] - sin_taps[t] * second_part[1]
        partner_im = partner_im + cos_taps[t] * second_part[1] + sin_taps[t] * second_part[0]
    product = jnp.stack(
        [
            master_re * partner_re + master_im * partner_im,
            master_im * partner_re - master_re * partner_im,
        ]
    )
    blocks = product.reshape(2, line_count // LOOK_AZ, LOOK_AZ, column_count // LOOK_RG, LOOK_RG)
    return jnp.mean(blocks, axis=(2, 4))


def shifted_pairs(
    arrived, resampled, range_shift, first_date, date_total, per_device, line_count, padded_width
):
    gathered = jnp.concatenate(arrived, axis=1)

    def one_pair(pair_index):
        within = pair_index // LAGS
        later = within + pair_index % LAGS + 1
        master = lax.dynamic_index_in_dim(resampled, within, 1, keepdims=False)
        partner = lax.dynamic_index_in_dim(gathered, later, 1, keepdims=False).reshape(
            2, line_count, padded_width
        )
        chosen = jnp.minimum(first_date + later, date_total - 1)
        band_gap = spectral_gap(range_shift, first_date + within, chosen)
        return pair_looks(master, partner, band_gap)

    looks = lax.map(one_pair, jnp.arange(per_device * LAGS, dtype=jnp.int32))
    looks = looks.reshape((per_device, LAGS) + looks.shape[1:])
    return jnp.transpose(looks, (2, 0, 1, 3, 4))


def body(slc, offsets, kernel_index, range_shift):
    with_lines = padded(slc, (("az", 2),), HALO_AZ)
    widened = padded(with_lines, (("rng", 3),), HALO_RG)
    per_device = slc.shape[1]
    line_count = slc.shape[2]
    column_count = slc.shape[3]
    padded_width = column_count + 2 * FILTER_HALF
    date_devices = lax.axis_size("date")
    first_date = lax.axis_index("date") * per_device
    date_total = date_devices * per_device
    resampled = jnp.stack(
        [resample(widened[:, 0], offsets[0], kernel_index[0], line_count, column_count)], axis=1
    )
    packed = resampled.reshape(2, per_device, line_count * padded_width)
    device_reach = (per_device - 1 + LAGS) // per_device
    arrived = [packed]
    current = packed
    for hop_count in range(device_reach):
        current = shifted(current, "date", -1)
        arrived.append(current)
    return shifted_pairs(
        arrived,
        resampled,
        range_shift,
        first_date,
        date_total,
        per_device,
        line_count,
        padded_width,
    )


def solution(mesh):
    return jax.shard_map(
        body,
        mesh=mesh,
        in_specs=(
            P(None, ("groups", "date"), "az", "rng"),
            P(("groups", "date"), None),
            P(("groups", "date"), None),
            P("groups"),
        ),
        out_specs=P(None, ("groups", "date"), None, "az", "rng"),
        check_vma=False,
    )
```

profile of v0, /device:TPU:0, one launch (start us, length us, event | category | flops | bytes accessed | tf_op | source)
XLA Modules:
  0.0 515.2 jit_solution(12337977733939594580)
XLA Ops:
  23.7 6.6 %fusion.7 = f32[2,39,2576]{2,1,0:T(8,128)S(1)} fusion(f32[2,39,2583]{2,1,0:T(8,128)S(1)} %bitcast_convert_fusion, f32[]{:T(128)} %bitcast.55, f32[]{:T(128)} %bitcast.54, f32[]{:T(128)} %bitcast.53, f32[]{:T(128)} %bitcast.52, f32[]{:T(128)} %bitcast.51, f32[]{:T(128)} %bitcast.50, f32[]{:T(128)} %bitcast.48, f32[]{:T(128)} %bitcast.41), kind=kLoop, calls=%fused_computation.64 | loop fusion | flops 3013920 | bytes 7233440 | tf_op jit(solution)/shard_map/add | solution.py:65
  30.3 5.5 %fusion.15 = bf16[2,32,2576]{2,1,0:T(8,128)(2,1)S(1)} fusion(f32[2,39,2576]{2,1,0:T(8,128)S(1)} %fusion.7, f32[]{:T(128)} %bitcast.62, f32[]{:T(128)} %bitcast.61, f32[]{:T(128)} %bitcast.60, f32[]{:T(128)} %bitcast.59, f32[]{:T(128)} %bitcast.58, f32[]{:T(128)} %bitcast.57, f32[]{:T(128)} %bitcast.56, f32[]{:T(128)} %bitcast.39), kind=kLoop, calls=%fused_computation.80 | loop fusion | flops 2637824 | bytes 5605408 | tf_op jit(solution)/shard_map/convert_element_type | solution.py:66
  38.0 5.5 %fusion.43 = bf16[2,1,32,2576]{3,2,0,1:T(8,128)(2,1)S(1)} fusion(f32[2,39,2576]{2,1,0:T(8,128)S(1)} %fusion.7, f32[]{:T(128)} %bitcast.62, f32[]{:T(128)} %bitcast.61, f32[]{:T(128)} %bitcast.60, f32[]{:T(128)} %bitcast.59, f32[]{:T(128)} %bitcast.58, f32[]{:T(128)} %bitcast.57, f32[]{:T(128)} %bitcast.56, f32[]{:T(128)} %bitcast.39), kind=kLoop, calls=%fused_computation.147 | loop fusion | flops 2637824 | bytes 5605408 | tf_op jit(solution)/shard_map/stack | solution.py:133
  49.9 9.2 %collective-permute-done.5 = bf16[2,1,82432]{2,0,1:T(2,128)(2,1)S(1)} collective-permute-done((bf16[2,1,82432]{2,0,1:T(2,128)(2,1)S(1)}, bf16[2,1,82432]{2,0,1:T(2,128)(2,1)S(1)}, u32[]{:S(2)}, u32[]{:S(2)}) %collective-permute-start.5) | collective-permute-done | bytes 329760 | tf_op jit(solution)/shard_map/ppermute | solution.py:35
  60.7 8.4 %collective-permute-done.6 = bf16[2,1,82432]{2,0,1:T(2,128)(2,1)S(1)} collective-permute-done((bf16[2,1,82432]{2,0,1:T(2,128)(2,1)S(1)}, bf16[2,1,82432]{2,0,1:T(2,128)(2,1)S(1)}, u32[]{:S(2)}, u32[]{:S(2)}) %collective-permute-start.6) | collective-permute-done | bytes 329760 | tf_op jit(solution)/shard_map/ppermute | solution.py:35
  70.6 7.5 %collective-permute-done.7 = bf16[2,1,82432]{2,0,1:T(2,128)(2,1)S(1)} collective-permute-done((bf16[2,1,82432]{2,0,1:T(2,128)(2,1)S(1)}, bf16[2,1,82432]{2,0,1:T(2,128)(2,1)S(1)}, u32[]{:S(2)}, u32[]{:S(2)}) %collective-permute-start.7) | collective-permute-done | bytes 329760 | tf_op jit(solution)/shard_map/ppermute | solution.py:35
  79.7 7.4 %collective-permute-done.8 = bf16[2,1,82432]{2,0,1:T(2,128)(2,1)S(1)} collective-permute-done((bf16[2,1,82432]{2,0,1:T(2,128)(2,1)S(1)}, bf16[2,1,82432]{2,0,1:T(2,128)(2,1)S(1)}, u32[]{:S(2)}, u32[]{:S(2)}) %collective-permute-start.8) | collective-permute-done | bytes 329760 | tf_op jit(solution)/shard_map/ppermute | solution.py:35
  88.7 8.6 %collective-permute-done.9 = bf16[2,1,82432]{2,0,1:T(2,128)(2,1)S(1)} collective-permute-done((bf16[2,1,82432]{2,0,1:T(2,128)(2,1)S(1)}, bf16[2,1,82432]{2,0,1:T(2,128)(2,1)S(1)}, u32[]{:S(2)}, u32[]{:S(2)}) %collective-permute-start.9) | collective-permute-done | bytes 329760 | tf_op jit(solution)/shard_map/ppermute | solution.py:35
  98.8 9.7 %collective-permute-done.10 = bf16[2,1,82432]{2,0,1:T(2,128)(2,1)S(1)} collective-permute-done((bf16[2,1,82432]{2,0,1:T(2,128)(2,1)S(1)}, bf16[2,1,82432]{2,0,1:T(2,128)(2,1)S(1)}, u32[]{:S(2)}, u32[]{:S(2)}) %collective-permute-start.10) | collective-permute-done | bytes 329760 | tf_op jit(solution)/shard_map/ppermute | solution.py:35
  110.2 7.2 %collective-permute-done.11 = bf16[2,1,82432]{2,0,1:T(2,128)(2,1)S(1)} collective-permute-done((bf16[2,1,82432]{2,0,1:T(2,128)(2,1)S(1)}, bf16[2,1,82432]{2,0,1:T(2,128)(2,1)S(1)}, u32[]{:S(2)}, u32[]{:S(2)}) %collective-permute-start.11) | collective-permute-done | bytes 329760 | tf_op jit(solution)/shard_map/ppermute | solution.py:35
  119.3 395.2 %while.12 = (s32[]{:T(128)}, f32[8,2,8,128]{3,2,0,1:T(8,128)S(1)}, s32[8]{0:T(128)S(1)}, s32[]{:T(128)}, f32[4]{0:T(128)S(1)}, /*index=5*/bf16[2,1,32,2576]{3,2,...) while((s32[]{:T(128)}, f32[8,2,8,128]{3,2,0,1:T(8,128)S(1)}, ...), condition=%wide.region_4.6_spmd, body=%wide.region_2.5_spmd.sunk | while | flops 28345088 | bytes 97682888 | solution.py:118
  123.9 5.0 slice_convert_fusion.36
  136.1 26.3 %multiply_add_fusion.9 = (f32[1,32,2560]{2,1,0:T(8,128)S(1)}, f32[1,32,2560]{2,1,0:T(8,128)S(1)}, f32[1,32,2560]{2,1,0:T(8,128)S(1)}, f32[1,32,2560]{2,1,0:T(8,128)S(1)}, f32[1,32,2560]{2,1,0:T(8,128)S(1)}) fusion(f32[2,32,2560]{2,1,0:T(8,128)S(1)} %get-tuple-element.339, f32[]{:T(128)} %bitcast.115, f32[]{:T(128)} %bitcast.116, ...), kind=kLoop, calls=%fused_computation.36.clone.1 | loop fusion | flops 22200320 | bytes 23920776 | tf_op jit(solution)/shard_map/while/body/eval_jaxpr/add | solution.py:94
  173.3 5.0 slice_convert_fusion.36
  185.5 26.3 %multiply_add_fusion.9 = (f32[1,32,2560]{2,1,0:T(8,128)S(1)}, f32[1,32,2560]{2,1,0:T(8,128)S(1)}, f32[1,32,2560]{2,1,0:T(8,128)S(1)}, f32[1,32,2560]{2,1,0:T(8,128)S(1)}, f32[1,32,2560]{2,1,0:T(8,128)S(1)}) fusion(f32[2,32,2560]{2,1,0:T(8,128)S(1)} %get-tuple-element.339, f32[]{:T(128)} %bitcast.115, f32[]{:T(128)} %bitcast.116, ...), kind=kLoop, calls=%fused_computation.36.clone.1 | loop fusion | flops 22200320 | bytes 23920776 | tf_op jit(solution)/shard_map/while/body/eval_jaxpr/add | solution.py:94
  234.9 26.3 %multiply_add_fusion.9 = (f32[1,32,2560]{2,1,0:T(8,128)S(1)}, f32[1,32,2560]{2,1,0:T(8,128)S(1)}, f32[1,32,2560]{2,1,0:T(8,128)S(1)}, f32[1,32,2560]{2,1,0:T(8,128)S(1)}, f32[1,32,2560]{2,1,0:T(8,128)S(1)}) fusion(f32[2,32,2560]{2,1,0:T(8,128)S(1)} %get-tuple-element.339, f32[]{:T(128)} %bitcast.115, f32[]{:T(128)} %bitcast.116, ...), kind=kLoop, calls=%fused_computation.36.clone.1 | loop fusion | flops 22200320 | bytes 23920776 | tf_op jit(solution)/shard_map/while/body/eval_jaxpr/add | solution.py:94
  272.1 5.0 slice_convert_fusion.36
  284.3 26.3 %multiply_add_fusion.9 = (f32[1,32,2560]{2,1,0:T(8,128)S(1)}, f32[1,32,2560]{2,1,0:T(8,128)S(1)}, f32[1,32,2560]{2,1,0:T(8,128)S(1)}, f32[1,32,2560]{2,1,0:T(8,128)S(1)}, f32[1,32,2560]{2,1,0:T(8,128)S(1)}) fusion(f32[2,32,2560]{2,1,0:T(8,128)S(1)} %get-tuple-element.339, f32[]{:T(128)} %bitcast.115, f32[]{:T(128)} %bitcast.116, ...), kind=kLoop, calls=%fused_computation.36.clone.1 | loop fusion | flops 22200320 | bytes 23920776 | tf_op jit(solution)/shard_map/while/body/eval_jaxpr/add | solution.py:94
  321.5 5.0 slice_convert_fusion.36
  333.7 26.3 %multiply_add_fusion.9 = (f32[1,32,2560]{2,1,0:T(8,128)S(1)}, f32[1,32,2560]{2,1,0:T(8,128)S(1)}, f32[1,32,2560]{2,1,0:T(8,128)S(1)}, f32[1,32,2560]{2,1,0:T(8,128)S(1)}, f32[1,32,2560]{2,1,0:T(8,128)S(1)}) fusion(f32[2,32,2560]{2,1,0:T(8,128)S(1)} %get-tuple-element.339, f32[]{:T(128)} %bitcast.115, f32[]{:T(128)} %bitcast.116, ...), kind=kLoop, calls=%fused_computation.36.clone.1 | loop fusion | flops 22200320 | bytes 23920776 | tf_op jit(solution)/shard_map/while/body/eval_jaxpr/add | solution.py:94
  370.9 5.0 slice_convert_fusion.36
  383.1 26.3 %multiply_add_fusion.9 = (f32[1,32,2560]{2,1,0:T(8,128)S(1)}, f32[1,32,2560]{2,1,0:T(8,128)S(1)}, f32[1,32,2560]{2,1,0:T(8,128)S(1)}, f32[1,32,2560]{2,1,0:T(8,128)S(1)}, f32[1,32,2560]{2,1,0:T(8,128)S(1)}) fusion(f32[2,32,2560]{2,1,0:T(8,128)S(1)} %get-tuple-element.339, f32[]{:T(128)} %bitcast.115, f32[]{:T(128)} %bitcast.116, ...), kind=kLoop, calls=%fused_computation.36.clone.1 | loop fusion | flops 22200320 | bytes 23920776 | tf_op jit(solution)/shard_map/while/body/eval_jaxpr/add | solution.py:94
  432.5 26.3 %multiply_add_fusion.9 = (f32[1,32,2560]{2,1,0:T(8,128)S(1)}, f32[1,32,2560]{2,1,0:T(8,128)S(1)}, f32[1,32,2560]{2,1,0:T(8,128)S(1)}, f32[1,32,2560]{2,1,0:T(8,128)S(1)}, f32[1,32,2560]{2,1,0:T(8,128)S(1)}) fusion(f32[2,32,2560]{2,1,0:T(8,128)S(1)} %get-tuple-element.339, f32[]{:T(128)} %bitcast.115, f32[]{:T(128)} %bitcast.116, ...), kind=kLoop, calls=%fused_computation.36.clone.1 | loop fusion | flops 22200320 | bytes 23920776 | tf_op jit(solution)/shard_map/while/body/eval_jaxpr/add | solution.py:94
  481.9 26.3 %multiply_add_fusion.9 = (f32[1,32,2560]{2,1,0:T(8,128)S(1)}, f32[1,32,2560]{2,1,0:T(8,128)S(1)}, f32[1,32,2560]{2,1,0:T(8,128)S(1)}, f32[1,32,2560]{2,1,0:T(8,128)S(1)}, f32[1,32,2560]{2,1,0:T(8,128)S(1)}) fusion(f32[2,32,2560]{2,1,0:T(8,128)S(1)} %get-tuple-element.339, f32[]{:T(128)} %bitcast.115, f32[]{:T(128)} %bitcast.116, ...), kind=kLoop, calls=%fused_computation.36.clone.1 | loop fusion | flops 22200320 | bytes 23920776 | tf_op jit(solution)/shard_map/while/body/eval_jaxpr/add | solution.py:94
  (379 shorter events, 169.5 us)
Async XLA Ops:
  1.0 10.5 %collective-permute-start = (bf16[2,1,12,2560]{3,2,0,1:T(8,128)(2,1)S(1)}, bf16[2,1,12,2560]{3,2,0,1:T(8,128)(2,1)S(1)}, u32[]{:S(2)}, u32[]{:S(2)}) collective-permute-start(bf16[2,1,12,2560]{3,2,0,1:T(8,128)(2,1)S(1)} %get-tuple-element.197), channel_id=1, source_target_pairs={{0,1},{2,3},{4,5},{6,7},{8,9},{10,11},{12,13},{14,15},{16,17},{18,... | collective-permute-start | bytes 368648 | tf_op jit(solution)/shard_map/ppermute | solution.py:23
  3.5 8.0 %collective-permute-start.1 = (bf16[2,1,12,2560]{3,2,0,1:T(8,128)(2,1)S(1)}, bf16[2,1,12,2560]{3,2,0,1:T(8,128)(2,1)S(1)}, u32[]{:S(2)}, u32[]{:S(2)}) collective-permute-start(bf16[2,1,12,2560]{3,2,0,1:T(8,128)(2,1)S(1)} %get-tuple-element.198), channel_id=1, source_target_pairs={{1,0},{3,2},{5,4},{7,6},{9,8},{11,10},{13,12},{15,14},{17,16},{19,... | collective-permute-start | bytes 368648 | tf_op jit(solution)/shard_map/ppermute | solution.py:25
  12.7 9.4 %collective-permute-start.2 = (bf16[2,1,56,36]{3,2,0,1:T(8,128)(2,1)S(1)}, bf16[2,1,56,36]{3,2,0,1:T(8,128)(2,1)S(1)}, u32[]{:S(2)}, u32[]{:S(2)}) collective-permute-start(bf16[2,1,56,36]{3,2,0,1:T(8,128)(2,1)S(1)} %get-tuple-element.196), channel_id=1, source_target_pairs={{0,2},{1,3},{4,6},{5,7},{8,10},{9,11},{12,14},{13,15},{16,18},{17,... | collective-permute-start | bytes 24200 | tf_op jit(solution)/shard_map/ppermute | solution.py:23
  16.9 6.0 %collective-permute-start.3 = (bf16[2,1,56,36]{3,2,0,1:T(8,128)(2,1)S(1)}, bf16[2,1,56,36]{3,2,0,1:T(8,128)(2,1)S(1)}, u32[]{:S(2)}, u32[]{:S(2)}) collective-permute-start(bf16[2,1,56,36]{3,2,0,1:T(8,128)(2,1)S(1)} %get-tuple-element.195), channel_id=1, source_target_pairs={{2,0},{3,1},{6,4},{7,5},{10,8},{11,9},{14,12},{15,13},{18,16},{19,... | collective-permute-start | bytes 24200 | tf_op jit(solution)/shard_map/ppermute | solution.py:25
  36.7 11.6 %collective-permute-start.4 = (bf16[2,1,82432]{2,0,1:T(2,128)(2,1)S(1)}, bf16[2,1,82432]{2,0,1:T(2,128)(2,1)S(1)}, u32[]{:S(2)}, u32[]{:S(2)}) collective-permute-start(bf16[2,1,82432]{2,0,1:T(2,128)(2,1)S(1)} %reshape_stack.3), channel_id=1, source_target_pairs={{4,0},{8,4},{12,8},{5,1},{9,5},{13,9},{6,2},{10,6},{14,10},{7,3},{... | collective-permute-start | bytes 989192 | tf_op jit(solution)/shard_map/ppermute | solution.py:35
  43.5 75.8 %copy-start.14 = (f32[4]{0:T(128)S(1)}, f32[4]{0:T(128)}, u32[]{:S(2)}) copy-start(f32[4]{0:T(128)} %param.10) | copy-start | bytes 52
  48.3 10.8 %collective-permute-start.5 = (bf16[2,1,82432]{2,0,1:T(2,128)(2,1)S(1)}, bf16[2,1,82432]{2,0,1:T(2,128)(2,1)S(1)}, u32[]{:S(2)}, u32[]{:S(2)}) collective-permute-start(bf16[2,1,82432]{2,0,1:T(2,128)(2,1)S(1)} %collective-permute-done.4), channel_id=1, source_target_pairs={{4,0},{8,4},{12,8},{5,1},{9,5},{13,9},{6,2},{10,6},{14,10},{7,3},{... | collective-permute-start | bytes 989192 | tf_op jit(solution)/shard_map/ppermute | solution.py:35
  59.1 9.9 %collective-permute-start.6 = (bf16[2,1,82432]{2,0,1:T(2,128)(2,1)S(1)}, bf16[2,1,82432]{2,0,1:T(2,128)(2,1)S(1)}, u32[]{:S(2)}, u32[]{:S(2)}) collective-permute-start(bf16[2,1,82432]{2,0,1:T(2,128)(2,1)S(1)} %collective-permute-done.5), channel_id=1, source_target_pairs={{4,0},{8,4},{12,8},{5,1},{9,5},{13,9},{6,2},{10,6},{14,10},{7,3},{... | collective-permute-start | bytes 989192 | tf_op jit(solution)/shard_map/ppermute | solution.py:35
  69.0 9.1 %collective-permute-start.7 = (bf16[2,1,82432]{2,0,1:T(2,128)(2,1)S(1)}, bf16[2,1,82432]{2,0,1:T(2,128)(2,1)S(1)}, u32[]{:S(2)}, u32[]{:S(2)}) collective-permute-start(bf16[2,1,82432]{2,0,1:T(2,128)(2,1)S(1)} %collective-permute-done.6), channel_id=1, source_target_pairs={{4,0},{8,4},{12,8},{5,1},{9,5},{13,9},{6,2},{10,6},{14,10},{7,3},{... | collective-permute-start | bytes 989192 | tf_op jit(solution)/shard_map/ppermute | solution.py:35
  78.1 9.0 %collective-permute-start.8 = (bf16[2,1,82432]{2,0,1:T(2,128)(2,1)S(1)}, bf16[2,1,82432]{2,0,1:T(2,128)(2,1)S(1)}, u32[]{:S(2)}, u32[]{:S(2)}) collective-permute-start(bf16[2,1,82432]{2,0,1:T(2,128)(2,1)S(1)} %collective-permute-done.7), channel_id=1, source_target_pairs={{4,0},{8,4},{12,8},{5,1},{9,5},{13,9},{6,2},{10,6},{14,10},{7,3},{... | collective-permute-start | bytes 989192 | tf_op jit(solution)/shard_map/ppermute | solution.py:35
  87.1 10.1 %collective-permute-start.9 = (bf16[2,1,82432]{2,0,1:T(2,128)(2,1)S(1)}, bf16[2,1,82432]{2,0,1:T(2,128)(2,1)S(1)}, u32[]{:S(2)}, u32[]{:S(2)}) collective-permute-start(bf16[2,1,82432]{2,0,1:T(2,128)(2,1)S(1)} %collective-permute-done.8), channel_id=1, source_target_pairs={{4,0},{8,4},{12,8},{5,1},{9,5},{13,9},{6,2},{10,6},{14,10},{7,3},{... | collective-permute-start | bytes 989192 | tf_op jit(solution)/shard_map/ppermute | solution.py:35
  97.2 11.3 %collective-permute-start.10 = (bf16[2,1,82432]{2,0,1:T(2,128)(2,1)S(1)}, bf16[2,1,82432]{2,0,1:T(2,128)(2,1)S(1)}, u32[]{:S(2)}, u32[]{:S(2)}) collective-permute-start(bf16[2,1,82432]{2,0,1:T(2,128)(2,1)S(1)} %collective-permute-done.9), channel_id=1, source_target_pairs={{4,0},{8,4},{12,8},{5,1},{9,5},{13,9},{6,2},{10,6},{14,10},{7,3},{... | collective-permute-start | bytes 989192 | tf_op jit(solution)/shard_map/ppermute | solution.py:35
  108.5 9.0 %collective-permute-start.11 = (bf16[2,1,82432]{2,0,1:T(2,128)(2,1)S(1)}, bf16[2,1,82432]{2,0,1:T(2,128)(2,1)S(1)}, u32[]{:S(2)}, u32[]{:S(2)}) collective-permute-start(bf16[2,1,82432]{2,0,1:T(2,128)(2,1)S(1)} %collective-permute-done.10), channel_id=1, source_target_pairs={{4,0},{8,4},{12,8},{5,1},{9,5},{13,9},{6,2},{10,6},{14,10},{7,3},{... | collective-permute-start | bytes 989192 | tf_op jit(solution)/shard_map/ppermute | solution.py:35
  132.5 3.4 copy-start.11
  132.5 3.6 copy-start.12
  181.9 3.6 copy-start.12
  231.3 3.4 copy-start.11
  231.3 3.6 copy-start.12
  280.7 3.4 copy-start.11
  280.7 3.6 copy-start.12
  330.1 3.6 copy-start.12
  379.5 3.6 copy-start.12
  428.9 3.6 copy-start.12
  478.3 3.6 copy-start.12
  (95 other events, 254.3 us)
where the time goes:
time: 519 us; the launch traced here: 515 us
  other arithmetic  294 us (57%)
  local copies, waits for them, and re-layouts  104 us (20%)
  waiting for transfers between devices  63.6 us (12%)
  loops' own time  30.7 us (6%)
  starting transfers between devices  19.6 us (4%)
    add x8, other arithmetic, pair_looks(): master_re * partner_re + master_im * partner_im  210 us
    ppermute x8, waiting for transfers between devices, shifted(): lax.ppermute(value, axis, [(source, source + steps) for source in range(l...  62.8 us
    another operation x32, local copies, waits for them, and re-layouts, pair_looks(): jnp.stack([master_re * partner_re + master_im * partner_im, master_im * p...  49.3 us
    convert_element_type x8, other arithmetic, pair_looks(): second_part = partner[:, :, t:t + column_count].astype(jnp.float32)  40.2 us
    another operation x1, loops' own time, shifted_pairs(): looks = lax.map(one_pair, jnp.arange(per_device * LAGS, dtype=jnp.int32))  30.7 us
    convert_element_type x8, other arithmetic, pair_looks(): first_part = master[:, :, t:t + column_count].astype(jnp.float32)  19.6 us
    ppermute x8, starting transfers between devices, shifted(): lax.ppermute(value, axis, [(source, source + steps) for source in range(l...  10.4 us
  transfers between devices with their start and end apart: 12, of which 9 were waited for; matrix products, arithmetic and copies ran while one was open for 3% of the time, Pallas kernels for 0%

commit v1 on v0

--- a/solution.py
+++ b/solution.py
@@ -1,6 +1,10 @@
+import functools
+
 import jax
 import jax.numpy as jnp
 from jax import lax
+from jax.experimental import pallas as pl
+from jax.experimental.pallas import tpu as pltpu
 from jax.sharding import PartitionSpec as P
 
 LAGS = 8
@@ -120,7 +124,348 @@
     return jnp.transpose(looks, (2, 0, 1, 3, 4))
 
 
+TILE = 128
+HALF_TILE = TILE // 2
+EDGE = 16
+MESH = pl.DeviceIdType.MESH
+
+
+def sinc_of(value):
+    angle = jnp.pi * value
+    nonzero = jnp.where(angle == 0.0, 1.0, angle)
+    return jnp.where(angle == 0.0, 1.0, jnp.sin(nonzero) / nonzero)
+
+
+def interpolation_shape(position):
+    return sinc_of(position) * (0.5 + 0.5 * jnp.cos(jnp.pi * position / 5.0))
+
+
+def halves(value):
+    high = value.astype(jnp.bfloat16)
+    low = (value - high.astype(jnp.float32)).astype(jnp.bfloat16)
+    return high, low
+
+
+def toeplitz(reversed_row):
+    spread = jnp.broadcast_to(reversed_row, (TILE, TILE))
+    rolled = pltpu.roll(spread, 0, 1, stride=1, stride_axis=0)
+    row = lax.broadcasted_iota(jnp.int32, (TILE, TILE), 0)
+    column = lax.broadcasted_iota(jnp.int32, (TILE, TILE), 1)
+    upper = jnp.where(row >= column, rolled, 0.0)
+    lower = jnp.where(row < column, rolled, 0.0)
+    return jnp.concatenate([upper, lower], axis=0)
+
+
+def fused_kernel(
+    dates,
+    lags,
+    offset_ref,
+    index_ref,
+    shift_ref,
+    slc_ref,
+    out_ref,
+    cells,
+    across,
+    outgoing,
+    bursts,
+    filters,
+    look_matrix,
+    products,
+    looks_out,
+    looks_in,
+    local_sem,
+    halo_send,
+    halo_recv,
+    burst_send,
+    burst_recv,
+    looks_send,
+    looks_recv,
+):
+    lines = slc_ref.shape[1]
+    columns = slc_ref.shape[2]
+    tiles = columns // TILE
+    spans = tiles + 1
+    share = lines // dates
+    groups = share // LOOK_AZ
+    az = lax.axis_index("az")
+    rng = lax.axis_index("rng")
+    date = lax.axis_index("date")
+
+    barrier = pltpu.get_barrier_semaphore()
+    peers = [{"az": 1 - az}, {"rng": 1 - rng}, {"az": 1 - az, "rng": 1 - rng}]
+    later = [lax.rem(date + k, dates) for k in range(dates)]
+    peers += [{"date": later[k]} for k in range(1, dates)]
+    for peer in peers:
+        pl.semaphore_signal(barrier, inc=1, device_id=peer, device_id_type=MESH)
+
+    own = pltpu.make_async_copy(
+        slc_ref, cells.at[:, pl.ds(EDGE, lines), pl.ds(TILE, columns)], local_sem
+    )
+    own.start()
+    pl.semaphore_wait(barrier, len(peers))
+
+    bottom = EDGE + lines
+    right = TILE + columns
+    from_line = pl.multiple_of((lines - EDGE) * (1 - az), EDGE)
+    to_line = pl.multiple_of(bottom * az, EDGE)
+    from_column = pl.multiple_of((columns - TILE) * (1 - rng), TILE)
+    to_column = pl.multiple_of(right * rng, TILE)
+    halo = []
+    for n, (source, target) in enumerate(
+        [
+            (
+                slc_ref.at[:, pl.ds(from_line, EDGE), :],
+                cells.at[:, pl.ds(to_line, EDGE), pl.ds(TILE, columns)],
+            ),
+            (
+                slc_ref.at[:, :, pl.ds(from_column, TILE)],
+                cells.at[:, pl.ds(EDGE, lines), pl.ds(to_column, TILE)],
+            ),
+            (
+                slc_ref.at[:, pl.ds(from_line, EDGE), pl.ds(from_column, TILE)],
+                cells.at[:, pl.ds(to_line, EDGE), pl.ds(to_column, TILE)],
+            ),
+        ]
+    ):
+        copy = pltpu.make_async_remote_copy(
+            src_ref=source,
+            dst_ref=target,
+            send_sem=halo_send.at[n],
+            recv_sem=halo_recv.at[n],
+            device_id=peers[n],
+            device_id_type=MESH,
+        )
+        copy.start()
+        halo.append(copy)
+
+    cells[:, pl.ds(to_line, EDGE), :] = jnp.zeros((2, EDGE, cells.shape[2]), jnp.bfloat16)
+    cells[:, :, pl.ds(to_column, TILE)] = jnp.zeros((2, cells.shape[1], TILE), jnp.bfloat16)
+
+    lane = lax.broadcasted_iota(jnp.int32, (8, TILE), 1)
+    reach = HALF_TILE - lane
+    tap = reach - offset_ref[0, 1] + 3
+    fraction = index_ref[0, 1].astype(jnp.float32) / KERNELS
+    shaped = interpolation_shape(tap.astype(jnp.float32) - 3.0 - fraction)
+    shaped = jnp.where((tap >= 0) & (tap < 8), shaped, 0.0)
+    column_taps = shaped / jnp.sum(shaped, axis=1, keepdims=True)
+    column_high, column_low = halves(toeplitz(column_taps[0:1]))
+    column_matrix = jnp.concatenate([column_high, column_low], axis=1)
+
+    position = lax.broadcasted_iota(jnp.int32, (8, TILE), 0).astype(jnp.float32) - 3.0
+    shaped = interpolation_shape(position - index_ref[0, 0].astype(jnp.float32) / KERNELS)
+    line_taps = shaped / jnp.sum(shaped, axis=0, keepdims=True)
+
+    own.wait()
+    for copy in halo:
+        copy.wait()
+
+    height = cells.shape[1]
+    for j in range(spans):
+        window = cells[:, :, j * TILE : (j + 2) * TILE].reshape(2 * height, 2 * TILE)
+        both = jnp.dot(window, column_matrix, preferred_element_type=jnp.float32)
+        both = both[:, :TILE] + both[:, TILE:]
+        across[0, j] = both[:height]
+        across[1, j] = both[height:]
+
+    def resampled_share(which):
+        start = EDGE - 3 + which * share + offset_ref[0, 0]
+        parts = []
+        for c in range(2):
+            total = None
+            for p in range(8):
+                term = line_taps[p : p + 1] * across[c, :, pl.ds(start + p, share), :]
+                total = term if total is None else total + term
+            parts.append(total)
+        return jnp.concatenate(parts, axis=1).astype(jnp.bfloat16)
+
+    copies = []
+    for k in range(1, dates):
+        outgoing[k - 1] = resampled_share(later[k])
+        copy = pltpu.make_async_remote_copy(
+            src_ref=outgoing.at[k - 1],
+            dst_ref=bursts.at[date],
+            send_sem=burst_send.at[k - 1],
+            recv_sem=burst_recv.at[k - 1],
+            device_id={"date": later[k]},
+            device_id_type=MESH,
+        )
+        copy.start()
+        copies.append(copy)
+    bursts[date] = resampled_share(date)
+
+    pairs = [(d, e) for d in range(dates) for e in range(d + 1, min(dates, d + lags + 1))]
+    sublane = lax.broadcasted_iota(jnp.int32, (8, TILE), 0)
+    spacing = reach.astype(jnp.float32)
+    window = 0.4 * sinc_of(0.4 * spacing)
+    window = window * (0.54 + 0.46 * jnp.cos(jnp.pi * spacing / (FILTER_HALF + 1)))
+    window = jnp.where(jnp.abs(reach) <= FILTER_HALF, window, 0.0)
+    for first in range(0, len(pairs), 8):
+        gaps = jnp.zeros((8, TILE), jnp.float32)
+        for n, (d, e) in enumerate(pairs[first : first + 8]):
+            gaps = jnp.where(sublane == n, shift_ref[d] - shift_ref[e], gaps)
+        phase = jnp.pi * gaps * spacing
+        even = window * jnp.cos(phase)
+        odd = window * jnp.sin(phase)
+        for n in range(len(pairs[first : first + 8])):
+            even_high, even_low = halves(toeplitz(even[n : n + 1]))
+            odd_high, odd_low = halves(toeplitz(odd[n : n + 1]))
+            filters[first + n, 0 : 2 * TILE, 0:TILE] = even_high
+            filters[first + n, 2 * TILE :, 0:TILE] = even_low
+            filters[first + n, 0 : 2 * TILE, TILE:] = odd_high
+            filters[first + n, 2 * TILE :, TILE:] = odd_low
+    for t in range(tiles):
+        column = t * TILE + lax.broadcasted_iota(jnp.int32, (TILE, TILE), 0)
+        look = LOOK_RG * lax.broadcasted_iota(jnp.int32, (TILE, TILE), 1)
+        inside = (column >= look) & (column < look + LOOK_RG)
+        look_matrix[t * TILE : (t + 1) * TILE, :] = jnp.where(inside, 1.0, 0.0).astype(
+            jnp.bfloat16
+        )
+
+    for copy in copies:
+        copy.wait_recv()
+
+    def filtered(which, n):
+        held = bursts[which]
+        paired = jnp.concatenate([held[:tiles], held[1:]], axis=2)
+        paired = paired.reshape(tiles * 2 * share, 2 * TILE)
+        total = jnp.dot(paired, filters[n, : 2 * TILE], preferred_element_type=jnp.float32)
+        total = total + jnp.dot(
+            paired, filters[n, 2 * TILE :], preferred_element_type=jnp.float32
+        )
+        total = total.reshape(tiles, 2 * share, 2 * TILE)
+        return (
+            total[:, :share, :TILE],
+            total[:, share:, :TILE],
+            total[:, :share, TILE:],
+            total[:, share:, TILE:],
+        )
+
+    rows = 2 * share
+    low_start = len(pairs) * rows
+    for n, (d, e) in enumerate(pairs):
+        even_re, even_im, odd_re, odd_im = filtered(d, n)
+        master_re = even_re + odd_im
+        master_im = even_im - odd_re
+        even_re, even_im, odd_re, odd_im = filtered(e, n)
+        partner_re = even_re - odd_im
+        partner_im = even_im + odd_re
+        product = jnp.concatenate(
+            [
+                master_re * partner_re + master_im * partner_im,
+                master_im * partner_re - master_re * partner_im,
+            ],
+            axis=1,
+        )
+        high, low = halves(product)
+        products[:, n * rows : (n + 1) * rows, :] = high
+        products[:, low_start + n * rows : low_start + (n + 1) * rows, :] = low
+
+    summed = None
+    for t in range(0, tiles, 2):
+        block = jnp.concatenate([products[t], products[t + 1]], axis=1)
+        term = jnp.dot(
+            block,
+            look_matrix[t * TILE : (t + 2) * TILE, :],
+            preferred_element_type=jnp.float32,
+        )
+        summed = term if summed is None else summed + term
+    summed = (summed[:low_start] + summed[low_start:]) / (LOOK_AZ * LOOK_RG)
+    total = summed
+    for m in range(1, LOOK_AZ):
+        total = total + pltpu.roll(summed, low_start - m, 0)
+
+    looks_out[...] = jnp.zeros(looks_out.shape, jnp.float32)
+    for n, (d, e) in enumerate(pairs):
+        for c in range(2):
+            for g in range(groups):
+                source = n * rows + c * share + g * LOOK_AZ
+                target = ((e - d - 1) * 2 + c) * groups + g
+                looks_out[d, target : target + 1, :] = total[source : source + 1]
+
+    returns = []
+    for k in range(1, dates):
+        copy = pltpu.make_async_remote_copy(
+            src_ref=looks_out.at[later[k]],
+            dst_ref=looks_in.at[date],
+            send_sem=looks_send.at[k - 1],
+            recv_sem=looks_recv.at[k - 1],
+            device_id={"date": later[k]},
+            device_id_type=MESH,
+        )
+        copy.start()
+        returns.append(copy)
+    looks_in[date] = looks_out[date]
+    out_ref[...] = jnp.zeros(out_ref.shape, jnp.float32)
+    for copy in returns:
+        copy.wait_recv()
+    for i in range(dates):
+        for j in range(lags):
+            for c in range(2):
+                source = (j * 2 + c) * groups
+                out_ref[c, j, i * groups : (i + 1) * groups, :] = looks_in[
+                    i, source : source + groups, :
+                ]
+    for copy in copies + returns:
+        copy.wait_send()
+
+
+def fused_fits(slc):
+    dates = lax.axis_size("date")
+    lines, columns = slc.shape[2], slc.shape[3]
+    return (
+        lax.axis_size("az") == 2
+        and lax.axis_size("rng") == 2
+        and slc.shape[1] == 1
+        and lines == 8 * dates
+        and lines >= 2 * EDGE
+        and columns == LOOK_RG * TILE
+        and 1 < dates <= LAGS
+    )
+
+
+def fused(slc, offsets, kernel_index, range_shift):
+    dates = lax.axis_size("date")
+    lags = min(LAGS, dates - 1)
+    lines, columns = slc.shape[2], slc.shape[3]
+    tiles = columns // TILE
+    spans = tiles + 1
+    share = lines // dates
+    groups = share // LOOK_AZ
+    pairs = sum(min(lags, dates - 1 - d) for d in range(dates))
+    look_rows = -(-lags * 2 * groups // 8) * 8
+    scratch = [
+        pltpu.VMEM((2, lines + 2 * EDGE, columns + 2 * TILE), jnp.bfloat16),
+        pltpu.VMEM((2, spans, lines + 2 * EDGE, TILE), jnp.float32),
+        pltpu.VMEM((dates - 1, spans, 2 * share, TILE), jnp.bfloat16),
+        pltpu.VMEM((dates, spans, 2 * share, TILE), jnp.bfloat16),
+        pltpu.VMEM((pairs, 4 * TILE, 2 * TILE), jnp.bfloat16),
+        pltpu.VMEM((columns, TILE), jnp.bfloat16),
+        pltpu.VMEM((tiles, 2 * pairs * 2 * share, TILE), jnp.bfloat16),
+        pltpu.VMEM((dates, look_rows, TILE), jnp.float32),
+        pltpu.VMEM((dates, look_rows, TILE), jnp.float32),
+        pltpu.SemaphoreType.DMA,
+        pltpu.SemaphoreType.DMA((3,)),
+        pltpu.SemaphoreType.DMA((3,)),
+        pltpu.SemaphoreType.DMA((dates - 1,)),
+        pltpu.SemaphoreType.DMA((dates - 1,)),
+        pltpu.SemaphoreType.DMA((dates - 1,)),
+        pltpu.SemaphoreType.DMA((dates - 1,)),
+    ]
+    smem = pl.BlockSpec(memory_space=pltpu.SMEM)
+    looks = pl.pallas_call(
+        functools.partial(fused_kernel, dates, lags),
+        out_shape=jax.ShapeDtypeStruct((2, LAGS, lines // LOOK_AZ, TILE), jnp.float32),
+        in_specs=[smem, smem, smem, pl.BlockSpec(memory_space=pl.ANY)],
+        out_specs=pl.BlockSpec(memory_space=pltpu.VMEM),
+        scratch_shapes=scratch,
+        compiler_params=pltpu.CompilerParams(collective_id=0, has_side_effects=True),
+    )(offsets, kernel_index, range_shift, slc.reshape(2, lines, columns))
+    return looks.reshape(2, 1, LAGS, lines // LOOK_AZ, TILE)
+
+
 def body(slc, offsets, kernel_index, range_shift):
+    if fused_fits(slc):
+        return fused(slc, offsets, kernel_index, range_shift)
     with_lines = padded(slc, (("az", 2),), HALO_AZ)
     widened = padded(with_lines, (("rng", 3),), HALO_RG)
     per_device = slc.shape[1]

time: 519 us -> 26.8 us (0.05)
  other arithmetic: 294 us -> 0 us
  local copies, waits for them, and re-layouts: 104 us -> 1.47 us
  waiting for transfers between devices: 63.6 us -> 0 us
  loops' own time: 30.7 us -> 0 us
  Pallas kernels: 0 us -> 25.2 us
  starting transfers between devices: 19.6 us -> 0 us
    add x9 -> x0, other arithmetic: 217 us -> none  [the longest x8 210 us: pair_looks(): master_re * partner_re + master_im * partner_im]
    convert_element_type x18 -> x0, other arithmetic: 65.5 us -> none  [the longest x8 40.2 us: pair_looks(): second_part = partner[:, :, t:t + column_count].astype(jnp.float32)]
    ppermute x12 -> x0, waiting for transfers between devices: 63.6 us -> none  [the longest x8 62.8 us: shifted(): lax.ppermute(value, axis, [(source, source + steps) for source in range(l...]
    another operation x33 -> x0, local copies, waits for them, and re-layouts: 49.9 us -> none  [the longest x32 49.3 us: pair_looks(): jnp.stack([master_re * partner_re + master_im * partner_im, master_im * p...]
    another operation x1 -> x0, loops' own time: 30.7 us -> none  [shifted_pairs(): looks = lax.map(one_pair, jnp.arange(per_device * LAGS, dtype=jnp.int32))]
    pallas_call x0 -> x1, Pallas kernels: none -> 25.2 us  [fused(): pl.pallas_call(functools.partial(fused_kernel, dates, lags), out_shape=ja...]
    ppermute x12 -> x0, starting transfers between devices: 19.6 us -> none  [the longest x8 10.4 us: shifted(): lax.ppermute(value, axis, [(source, source + steps) for source in range(l...]
    dynamic_slice x24 -> x0, local copies, waits for them, and re-layouts: 19.5 us -> none  [the longest x8 9.65 us: one_pair(): lax.dynamic_index_in_dim(gathered, later, 1, keepdims=False)]
  transfers between devices with their start and end apart: 12 -> 0, of which waited for: 9 -> 0; matrix products, arithmetic and copies ran while one was open for 3% -> 0% of each run, Pallas kernels for 0% -> 0%
where the time goes in v1:
time: 26.8 us; the launch traced here: 26.7 us
  Pallas kernels  25.2 us (94%)
  local copies, waits for them, and re-layouts  1.47 us (5%)
    pallas_call x1, Pallas kernels, fused(): pl.pallas_call(functools.partial(fused_kernel, dates, lags), out_shape=ja...  25.2 us
    unnamed x1, local copies, waits for them, and re-layouts  1.47 us

profile of v1, /device:TPU:0, one launch (start us, length us, event | category | flops | bytes accessed | tf_op | source)
XLA Modules:
  0.0 26.7 jit_solution(16273964007709393920)
XLA Ops:
  0.0 25.2 %shard_map.46 = f32[2,8,8,128]{3,2,1,0:T(8,128)} custom-call(s32[1,2]{1,0:T(1,128)} %offset_ref.1, s32[1,2]{1,0:T(1,128)} %index_ref.1, f32[4]{0:T(128)} %shift_ref.1, bf16[2,32,2560]{2,1,0:T(8,128)(2,1)} %bitcast.4), custom_call_target="tpu_custom_call" | custom-call | tf_op jit(solution)/shard_map/pallas_call | solution.py:455
  25.2 1.5 %copy.7 = f32[2,1,8,8,128]{4,3,2,1,0:T(8,128)} copy(f32[2,1,8,8,128]{4,3,2,1,0:T(8,128)} %bitcast.5) | data formatting | bytes 131072

commit v2 on v1

--- a/solution.py
+++ b/solution.py
@@ -156,23 +156,37 @@
     return jnp.concatenate([upper, lower], axis=0)
 
 
+def flipped(value, mask):
+    bit = 1
+    result = value
+    while bit <= mask:
+        if mask & bit:
+            result = result + bit * (1 - 2 * lax.rem(value // bit, 2))
+        bit *= 2
+    return result
+
+
 def fused_kernel(
     dates,
     lags,
+    segments,
+    offset_hbm,
+    index_hbm,
+    shift_hbm,
+    slc_ref,
+    out_ref,
     offset_ref,
     index_ref,
     shift_ref,
-    slc_ref,
-    out_ref,
     cells,
     across,
     outgoing,
     bursts,
     filters,
     look_matrix,
-    products,
     looks_out,
     looks_in,
+    small_sem,
     local_sem,
     halo_send,
     halo_recv,
@@ -180,6 +194,8 @@
     burst_recv,
     looks_send,
     looks_recv,
+    rising,
+    falling,
 ):
     lines = slc_ref.shape[1]
     columns = slc_ref.shape[2]
@@ -193,23 +209,42 @@
 
     barrier = pltpu.get_barrier_semaphore()
     peers = [{"az": 1 - az}, {"rng": 1 - rng}, {"az": 1 - az, "rng": 1 - rng}]
-    later = [lax.rem(date + k, dates) for k in range(dates)]
-    peers += [{"date": later[k]} for k in range(1, dates)]
     for peer in peers:
         pl.semaphore_signal(barrier, inc=1, device_id=peer, device_id_type=MESH)
 
+    @pl.when(date > 0)
+    def _():
+        pl.semaphore_signal(barrier, inc=1, device_id={"date": date - 1}, device_id_type=MESH)
+
+    @pl.when(date < dates - 1)
+    def _():
+        pl.semaphore_signal(barrier, inc=1, device_id={"date": date + 1}, device_id_type=MESH)
+
+    small = [
+        pltpu.make_async_copy(source, target, small_sem.at[n])
+        for n, (source, target) in enumerate(
+            [(offset_hbm, offset_ref), (index_hbm, index_ref), (shift_hbm, shift_ref)]
+        )
+    ]
+    for copy in small:
+        copy.start()
     own = pltpu.make_async_copy(
         slc_ref, cells.at[:, pl.ds(EDGE, lines), pl.ds(TILE, columns)], local_sem
     )
     own.start()
-    pl.semaphore_wait(barrier, len(peers))
 
     bottom = EDGE + lines
     right = TILE + columns
     from_line = pl.multiple_of((lines - EDGE) * (1 - az), EDGE)
     to_line = pl.multiple_of(bottom * az, EDGE)
+    edge_line = pl.multiple_of(bottom * (1 - az), EDGE)
     from_column = pl.multiple_of((columns - TILE) * (1 - rng), TILE)
     to_column = pl.multiple_of(right * rng, TILE)
+    cells[:, :, pl.ds(to_column, TILE)] = jnp.zeros((2, cells.shape[1], TILE), jnp.bfloat16)
+    across[:, :, pl.ds(to_line, EDGE), :] = jnp.zeros((2, spans, EDGE, TILE), jnp.float32)
+
+    inner = jnp.where((date > 0) & (date < dates - 1), 1, 0)
+    pl.semaphore_wait(barrier, len(peers) + 1 + inner)
     halo = []
     for n, (source, target) in enumerate(
         [
@@ -238,9 +273,16 @@
         copy.start()
         halo.append(copy)
 
-    cells[:, pl.ds(to_line, EDGE), :] = jnp.zeros((2, EDGE, cells.shape[2]), jnp.bfloat16)
-    cells[:, :, pl.ds(to_column, TILE)] = jnp.zeros((2, cells.shape[1], TILE), jnp.bfloat16)
-
+    @pl.when(date == 0)
+    def _():
+        pl.semaphore_signal(rising, inc=1, device_id={"date": date + 1}, device_id_type=MESH)
+
+    @pl.when(date == dates - 1)
+    def _():
+        pl.semaphore_signal(falling, inc=1, device_id={"date": date - 1}, device_id_type=MESH)
+
+    for copy in small:
+        copy.wait()
     lane = lax.broadcasted_iota(jnp.int32, (8, TILE), 1)
     reach = HALF_TILE - lane
     tap = reach - offset_ref[0, 1] + 3
@@ -255,43 +297,78 @@
     shaped = interpolation_shape(position - index_ref[0, 0].astype(jnp.float32) / KERNELS)
     line_taps = shaped / jnp.sum(shaped, axis=0, keepdims=True)
 
+    def range_pass(start, height, which):
+        window = jnp.concatenate(
+            [
+                cells[:, pl.ds(start, height), j * TILE : (j + 2) * TILE].reshape(
+                    2 * height, 2 * TILE
+                )
+                for j in which
+            ],
+            axis=0,
+        )
+        both = jnp.dot(window, column_matrix, preferred_element_type=jnp.float32)
+        both = (both[:, :TILE] + both[:, TILE:]).reshape(len(which), 2, height, TILE)
+        for n, j in enumerate(which):
+            for c in range(2):
+                across[c, j, pl.ds(start, height), :] = both[n, c]
+
     own.wait()
+    range_pass(EDGE, lines, range(1, spans - 1))
+
+    @pl.when(date > 0)
+    def _():
+        pl.semaphore_wait(rising, 1)
+
+    @pl.when((date > 0) & (date < dates - 1))
+    def _():
+        pl.semaphore_signal(rising, inc=1, device_id={"date": date + 1}, device_id_type=MESH)
+
+    @pl.when(date < dates - 1)
+    def _():
+        pl.semaphore_wait(falling, 1)
+
+    @pl.when((date > 0) & (date < dates - 1))
+    def _():
+        pl.semaphore_signal(falling, inc=1, device_id={"date": date - 1}, device_id_type=MESH)
+
     for copy in halo:
-        copy.wait()
-
-    height = cells.shape[1]
-    for j in range(spans):
-        window = cells[:, :, j * TILE : (j + 2) * TILE].reshape(2 * height, 2 * TILE)
-        both = jnp.dot(window, column_matrix, preferred_element_type=jnp.float32)
-        both = both[:, :TILE] + both[:, TILE:]
-        across[0, j] = both[:height]
-        across[1, j] = both[height:]
-
-    def resampled_share(which):
+        copy.wait_recv()
+    range_pass(EDGE, lines, [0, spans - 1])
+
+    def resampled_share(which, low, high):
         start = EDGE - 3 + which * share + offset_ref[0, 0]
         parts = []
         for c in range(2):
             total = None
             for p in range(8):
-                term = line_taps[p : p + 1] * across[c, :, pl.ds(start + p, share), :]
+                term = line_taps[p : p + 1] * across[c, low:high, pl.ds(start + p, share), :]
                 total = term if total is None else total + term
             parts.append(total)
         return jnp.concatenate(parts, axis=1).astype(jnp.bfloat16)
 
-    copies = []
-    for k in range(1, dates):
-        outgoing[k - 1] = resampled_share(later[k])
-        copy = pltpu.make_async_remote_copy(
-            src_ref=outgoing.at[k - 1],
-            dst_ref=bursts.at[date],
-            send_sem=burst_send.at[k - 1],
-            recv_sem=burst_recv.at[k - 1],
-            device_id={"date": later[k]},
-            device_id_type=MESH,
-        )
-        copy.start()
-        copies.append(copy)
-    bursts[date] = resampled_share(date)
+    width = tiles // segments
+    partners = [flipped(date, mask) for mask in range(dates - 1, 0, -1)]
+    sent = []
+    for s in range(segments):
+        low = 0 if s == 0 else s * width + 1
+        high = (s + 1) * width + 1
+        range_pass(edge_line, EDGE, range(low, high))
+        arriving = []
+        for n, partner in enumerate(partners):
+            outgoing[n, low:high] = resampled_share(partner, low, high)
+            copy = pltpu.make_async_remote_copy(
+                src_ref=outgoing.at[n, low:high],
+                dst_ref=bursts.at[date, low:high],
+                send_sem=burst_send.at[s, n],
+                recv_sem=burst_recv.at[s, n],
+                device_id={"date": partner},
+                device_id_type=MESH,
+            )
+            copy.start()
+            arriving.append(copy)
+        bursts[date, low:high] = resampled_share(date, low, high)
+        sent.append(arriving)
 
     pairs = [(d, e) for d in range(dates) for e in range(d + 1, min(dates, d + lags + 1))]
     sublane = lax.broadcasted_iota(jnp.int32, (8, TILE), 0)
@@ -320,61 +397,60 @@
         look_matrix[t * TILE : (t + 1) * TILE, :] = jnp.where(inside, 1.0, 0.0).astype(
             jnp.bfloat16
         )
-
-    for copy in copies:
-        copy.wait_recv()
-
-    def filtered(which, n):
-        held = bursts[which]
-        paired = jnp.concatenate([held[:tiles], held[1:]], axis=2)
-        paired = paired.reshape(tiles * 2 * share, 2 * TILE)
-        total = jnp.dot(paired, filters[n, : 2 * TILE], preferred_element_type=jnp.float32)
-        total = total + jnp.dot(
-            paired, filters[n, 2 * TILE :], preferred_element_type=jnp.float32
-        )
-        total = total.reshape(tiles, 2 * share, 2 * TILE)
-        return (
-            total[:, :share, :TILE],
-            total[:, share:, :TILE],
-            total[:, :share, TILE:],
-            total[:, share:, TILE:],
-        )
+    looks_out[...] = jnp.zeros(looks_out.shape, jnp.float32)
+    out_ref[...] = jnp.zeros(out_ref.shape, jnp.float32)
 
     rows = 2 * share
-    low_start = len(pairs) * rows
-    for n, (d, e) in enumerate(pairs):
-        even_re, even_im, odd_re, odd_im = filtered(d, n)
-        master_re = even_re + odd_im
-        master_im = even_im - odd_re
-        even_re, even_im, odd_re, odd_im = filtered(e, n)
-        partner_re = even_re - odd_im
-        partner_im = even_im + odd_re
-        product = jnp.concatenate(
-            [
-                master_re * partner_re + master_im * partner_im,
-                master_im * partner_re - master_re * partner_im,
-            ],
-            axis=1,
-        )
-        high, low = halves(product)
-        products[:, n * rows : (n + 1) * rows, :] = high
-        products[:, low_start + n * rows : low_start + (n + 1) * rows, :] = low
-
     summed = None
-    for t in range(0, tiles, 2):
-        block = jnp.concatenate([products[t], products[t + 1]], axis=1)
-        term = jnp.dot(
-            block,
-            look_matrix[t * TILE : (t + 2) * TILE, :],
-            preferred_element_type=jnp.float32,
-        )
-        summed = term if summed is None else summed + term
-    summed = (summed[:low_start] + summed[low_start:]) / (LOOK_AZ * LOOK_RG)
+    for s in range(segments):
+        for copy in sent[s]:
+            copy.wait_recv()
+        low, high = s * width, (s + 1) * width
+        windows = []
+        for d in range(dates):
+            held = bursts[d, low : high + 1]
+            paired = jnp.concatenate([held[:width], held[1:]], axis=2)
+            windows.append(paired.reshape(width * rows, 2 * TILE))
+        highs, lows = [], []
+        for n, (d, e) in enumerate(pairs):
+            both = jnp.concatenate([windows[d], windows[e]], axis=0)
+            total = jnp.dot(both, filters[n, : 2 * TILE], preferred_element_type=jnp.float32)
+            total = total + jnp.dot(
+                both, filters[n, 2 * TILE :], preferred_element_type=jnp.float32
+            )
+            total = total.reshape(2, width, rows, 2 * TILE)
+            even_re, even_im = total[:, :, :share, :TILE], total[:, :, share:, :TILE]
+            odd_re, odd_im = total[:, :, :share, TILE:], total[:, :, share:, TILE:]
+            master_re = even_re[0] + odd_im[0]
+            master_im = even_im[0] - odd_re[0]
+            partner_re = even_re[1] - odd_im[1]
+            partner_im = even_im[1] + odd_re[1]
+            product = jnp.concatenate(
+                [
+                    master_re * partner_re + master_im * partner_im,
+                    master_im * partner_re - master_re * partner_im,
+                ],
+                axis=1,
+            )
+            upper, lower = halves(product)
+            highs.append(upper)
+            lows.append(lower)
+        stacked = jnp.concatenate(highs + lows, axis=1)
+        for t in range(0, width, 2):
+            step = min(2, width - t)
+            block = jnp.concatenate([stacked[t + i] for i in range(step)], axis=1)
+            term = jnp.dot(
+                block,
+                look_matrix[(low + t) * TILE : (low + t + step) * TILE, :],
+                preferred_element_type=jnp.float32,
+            )
+            summed = term if summed is None else summed + term
+
+    middle = len(pairs) * rows
+    summed = (summed[:middle] + summed[middle:]) / (LOOK_AZ * LOOK_RG)
     total = summed
     for m in range(1, LOOK_AZ):
-        total = total + pltpu.roll(summed, low_start - m, 0)
-
-    looks_out[...] = jnp.zeros(looks_out.shape, jnp.float32)
+        total = total + pltpu.roll(summed, middle - m, 0)
     for n, (d, e) in enumerate(pairs):
         for c in range(2):
             for g in range(groups):
@@ -383,19 +459,21 @@
                 looks_out[d, target : target + 1, :] = total[source : source + 1]
 
     returns = []
-    for k in range(1, dates):
+    for n, partner in enumerate(partners):
         copy = pltpu.make_async_remote_copy(
-            src_ref=looks_out.at[later[k]],
+            src_ref=looks_out.at[partner],
             dst_ref=looks_in.at[date],
-            send_sem=looks_send.at[k - 1],
-            recv_sem=looks_recv.at[k - 1],
-            device_id={"date": later[k]},
+            send_sem=looks_send.at[n],
+            recv_sem=looks_recv.at[n],
+            device_id={"date": partner},
             device_id_type=MESH,
         )
         copy.start()
         returns.append(copy)
     looks_in[date] = looks_out[date]
-    out_ref[...] = jnp.zeros(out_ref.shape, jnp.float32)
+    for arriving in [halo] + sent:
+        for copy in arriving:
+            copy.wait_send()
     for copy in returns:
         copy.wait_recv()
     for i in range(dates):
@@ -405,7 +483,7 @@
                 out_ref[c, j, i * groups : (i + 1) * groups, :] = looks_in[
                     i, source : source + groups, :
                 ]
-    for copy in copies + returns:
+    for copy in returns:
         copy.wait_send()
 
 
@@ -419,7 +497,7 @@
         and lines == 8 * dates
         and lines >= 2 * EDGE
         and columns == LOOK_RG * TILE
-        and 1 < dates <= LAGS
+        and dates in (2, 4, 8)
     )
 
 
@@ -433,29 +511,35 @@
     groups = share // LOOK_AZ
     pairs = sum(min(lags, dates - 1 - d) for d in range(dates))
     look_rows = -(-lags * 2 * groups // 8) * 8
+    segments = 4 if tiles % 4 == 0 else 1
     scratch = [
+        pltpu.SMEM(offsets.shape, offsets.dtype),
+        pltpu.SMEM(kernel_index.shape, kernel_index.dtype),
+        pltpu.SMEM(range_shift.shape, range_shift.dtype),
         pltpu.VMEM((2, lines + 2 * EDGE, columns + 2 * TILE), jnp.bfloat16),
         pltpu.VMEM((2, spans, lines + 2 * EDGE, TILE), jnp.float32),
         pltpu.VMEM((dates - 1, spans, 2 * share, TILE), jnp.bfloat16),
         pltpu.VMEM((dates, spans, 2 * share, TILE), jnp.bfloat16),
         pltpu.VMEM((pairs, 4 * TILE, 2 * TILE), jnp.bfloat16),
         pltpu.VMEM((columns, TILE), jnp.bfloat16),
-        pltpu.VMEM((tiles, 2 * pairs * 2 * share, TILE), jnp.bfloat16),
         pltpu.VMEM((dates, look_rows, TILE), jnp.float32),
         pltpu.VMEM((dates, look_rows, TILE), jnp.float32),
+        pltpu.SemaphoreType.DMA((3,)),
         pltpu.SemaphoreType.DMA,
         pltpu.SemaphoreType.DMA((3,)),
         pltpu.SemaphoreType.DMA((3,)),
+        pltpu.SemaphoreType.DMA((segments, dates - 1)),
+        pltpu.SemaphoreType.DMA((segments, dates - 1)),
         pltpu.SemaphoreType.DMA((dates - 1,)),
         pltpu.SemaphoreType.DMA((dates - 1,)),
-        pltpu.SemaphoreType.DMA((dates - 1,)),
-        pltpu.SemaphoreType.DMA((dates - 1,)),
+        pltpu.SemaphoreType.REGULAR,
+        pltpu.SemaphoreType.REGULAR,
     ]
-    smem = pl.BlockSpec(memory_space=pltpu.SMEM)
+    anywhere = pl.BlockSpec(memory_space=pl.ANY)
     looks = pl.pallas_call(
-        functools.partial(fused_kernel, dates, lags),
+        functools.partial(fused_kernel, dates, lags, segments),
         out_shape=jax.ShapeDtypeStruct((2, LAGS, lines // LOOK_AZ, TILE), jnp.float32),
-        in_specs=[smem, smem, smem, pl.BlockSpec(memory_space=pl.ANY)],
+        in_specs=[anywhere] * 4,
         out_specs=pl.BlockSpec(memory_space=pltpu.VMEM),
         scratch_shapes=scratch,
         compiler_params=pltpu.CompilerParams(collective_id=0, has_side_effects=True),

time: 26.8 us -> 24 us (0.90)
  Pallas kernels: 25.2 us -> 22.4 us
    pallas_call x1, Pallas kernels: 25.2 us -> 22.4 us  [fused(): pl.pallas_call(functools.partial(fused_kernel, dates, lags, segments), ou...]
where the time goes in v2:
time: 24 us; the launch traced here: 23.9 us
  Pallas kernels  22.4 us (93%)
  local copies, waits for them, and re-layouts  1.47 us (6%)
    pallas_call x1, Pallas kernels, fused(): pl.pallas_call(functools.partial(fused_kernel, dates, lags, segments), ou...  22.4 us
    unnamed x1, local copies, waits for them, and re-layouts  1.47 us

profile of v2, /device:TPU:0, one launch (start us, length us, event | category | flops | bytes accessed | tf_op | source)
XLA Modules:
  0.0 23.9 jit_solution(8919141135406072608)
XLA Ops:
  0.0 22.4 %shard_map.46 = f32[2,8,8,128]{3,2,1,0:T(8,128)} custom-call(s32[1,2]{1,0:T(1,128)} %offset_hbm.1, s32[1,2]{1,0:T(1,128)} %index_hbm.1, f32[4]{0:T(128)} %shift_hbm.1, bf16[2,32,2560]{2,1,0:T(8,128)(2,1)} %bitcast.4), custom_call_target="tpu_custom_call" | custom-call | tf_op jit(solution)/shard_map/pallas_call | solution.py:539
  22.4 1.5 %copy.7 = f32[2,1,8,8,128]{4,3,2,1,0:T(8,128)} copy(f32[2,1,8,8,128]{4,3,2,1,0:T(8,128)} %bitcast.5) | data formatting | bytes 131072

commit v3 on v2

--- a/solution.py
+++ b/solution.py
@@ -156,6 +156,12 @@
     return jnp.concatenate([upper, lower], axis=0)
 
 
+def segment_cuts(tiles):
+    if tiles < 8:
+        return [tiles]
+    return [tiles // 4, tiles * 11 // 20, tiles * 17 // 20, tiles]
+
+
 def flipped(value, mask):
     bit = 1
     result = value
@@ -169,7 +175,6 @@
 def fused_kernel(
     dates,
     lags,
-    segments,
     offset_hbm,
     index_hbm,
     shift_hbm,
@@ -206,6 +211,7 @@
     az = lax.axis_index("az")
     rng = lax.axis_index("rng")
     date = lax.axis_index("date")
+    cuts = segment_cuts(tiles)
 
     barrier = pltpu.get_barrier_semaphore()
     peers = [{"az": 1 - az}, {"rng": 1 - rng}, {"az": 1 - az, "rng": 1 - rng}]
@@ -245,42 +251,50 @@
 
     inner = jnp.where((date > 0) & (date < dates - 1), 1, 0)
     pl.semaphore_wait(barrier, len(peers) + 1 + inner)
+    pieces = [
+        (
+            slc_ref.at[:, :, pl.ds(from_column, TILE)],
+            cells.at[:, pl.ds(EDGE, lines), pl.ds(to_column, TILE)],
+            peers[1],
+        ),
+        (
+            slc_ref.at[:, pl.ds(from_line, EDGE), pl.ds(from_column, TILE)],
+            cells.at[:, pl.ds(to_line, EDGE), pl.ds(to_column, TILE)],
+            peers[2],
+        ),
+    ]
+    for s, (first, last) in enumerate(zip([0] + cuts[:-1], cuts)):
+        extent = (last - first) * TILE
+        piece = (
+            slc_ref.at[:, pl.ds(from_line, EDGE), pl.ds(first * TILE, extent)],
+            cells.at[:, pl.ds(to_line, EDGE), pl.ds((first + 1) * TILE, extent)],
+            peers[0],
+        )
+        pieces.insert(s if s == 0 else len(pieces), piece)
     halo = []
-    for n, (source, target) in enumerate(
-        [
-            (
-                slc_ref.at[:, pl.ds(from_line, EDGE), :],
-                cells.at[:, pl.ds(to_line, EDGE), pl.ds(TILE, columns)],
-            ),
-            (
-                slc_ref.at[:, :, pl.ds(from_column, TILE)],
-                cells.at[:, pl.ds(EDGE, lines), pl.ds(to_column, TILE)],
-            ),
-            (
-                slc_ref.at[:, pl.ds(from_line, EDGE), pl.ds(from_column, TILE)],
-                cells.at[:, pl.ds(to_line, EDGE), pl.ds(to_column, TILE)],
-            ),
-        ]
-    ):
+    for n, (source, target, peer) in enumerate(pieces):
         copy = pltpu.make_async_remote_copy(
             src_ref=source,
             dst_ref=target,
             send_sem=halo_send.at[n],
             recv_sem=halo_recv.at[n],
-            device_id=peers[n],
+            device_id=peer,
             device_id_type=MESH,
         )
         copy.start()
         halo.append(copy)
 
-    @pl.when(date == 0)
-    def _():
-        pl.semaphore_signal(rising, inc=1, device_id={"date": date + 1}, device_id_type=MESH)
-
-    @pl.when(date == dates - 1)
-    def _():
-        pl.semaphore_signal(falling, inc=1, device_id={"date": date - 1}, device_id_type=MESH)
-
+    def relay(step):
+        @pl.when((date >= step) & (date < dates - 1))
+        def _():
+            pl.semaphore_signal(rising, inc=1, device_id={"date": date + 1}, device_id_type=MESH)
+
+        @pl.when((date <= dates - 1 - step) & (date > 0))
+        def _():
+            pl.semaphore_signal(falling, inc=1, device_id={"date": date - 1}, device_id_type=MESH)
+
+    if dates > 2:
+        relay(1)
     for copy in small:
         copy.wait()
     lane = lax.broadcasted_iota(jnp.int32, (8, TILE), 1)
@@ -316,25 +330,18 @@
     own.wait()
     range_pass(EDGE, lines, range(1, spans - 1))
 
-    @pl.when(date > 0)
-    def _():
-        pl.semaphore_wait(rising, 1)
-
-    @pl.when((date > 0) & (date < dates - 1))
-    def _():
-        pl.semaphore_signal(rising, inc=1, device_id={"date": date + 1}, device_id_type=MESH)
-
-    @pl.when(date < dates - 1)
-    def _():
-        pl.semaphore_wait(falling, 1)
-
-    @pl.when((date > 0) & (date < dates - 1))
-    def _():
-        pl.semaphore_signal(falling, inc=1, device_id={"date": date - 1}, device_id_type=MESH)
-
-    for copy in halo:
-        copy.wait_recv()
-    range_pass(EDGE, lines, [0, spans - 1])
+    for step in range(1, dates - 1):
+
+        @pl.when(date >= step + 1)
+        def _():
+            pl.semaphore_wait(rising, 1)
+
+        @pl.when(date < dates - 1 - step)
+        def _():
+            pl.semaphore_wait(falling, 1)
+
+        if step < dates - 2:
+            relay(step + 1)
 
     def resampled_share(which, low, high):
         start = EDGE - 3 + which * share + offset_ref[0, 0]
@@ -347,12 +354,18 @@
             parts.append(total)
         return jnp.concatenate(parts, axis=1).astype(jnp.bfloat16)
 
-    width = tiles // segments
-    partners = [flipped(date, mask) for mask in range(dates - 1, 0, -1)]
+    masks = [dates // 2] + [m for m in range(dates - 1, 0, -1) if m != dates // 2]
+    partners = [flipped(date, mask) for mask in masks]
+    bounds = [0] + cuts[:-1] + [spans]
     sent = []
-    for s in range(segments):
-        low = 0 if s == 0 else s * width + 1
-        high = (s + 1) * width + 1
+    for s in range(len(cuts)):
+        low, high = bounds[s], bounds[s + 1]
+        for copy in halo[:3] if s == 0 else halo[s + 2 : s + 3]:
+            copy.wait_recv()
+        if s == 0:
+            range_pass(EDGE, lines, [0])
+        if high == spans:
+            range_pass(EDGE, lines, [spans - 1])
         range_pass(edge_line, EDGE, range(low, high))
         arriving = []
         for n, partner in enumerate(partners):
@@ -402,10 +415,11 @@
 
     rows = 2 * share
     summed = None
-    for s in range(segments):
+    for s in range(len(cuts)):
         for copy in sent[s]:
             copy.wait_recv()
-        low, high = s * width, (s + 1) * width
+        low, high = max(bounds[s] - 1, 0), bounds[s + 1] - 1
+        width = high - low
         windows = []
         for d in range(dates):
             held = bursts[d, low : high + 1]
@@ -511,7 +525,7 @@
     groups = share // LOOK_AZ
     pairs = sum(min(lags, dates - 1 - d) for d in range(dates))
     look_rows = -(-lags * 2 * groups // 8) * 8
-    segments = 4 if tiles % 4 == 0 else 1
+    segments = len(segment_cuts(tiles))
     scratch = [
         pltpu.SMEM(offsets.shape, offsets.dtype),
         pltpu.SMEM(kernel_index.shape, kernel_index.dtype),
@@ -526,8 +540,8 @@
         pltpu.VMEM((dates, look_rows, TILE), jnp.float32),
         pltpu.SemaphoreType.DMA((3,)),
         pltpu.SemaphoreType.DMA,
-        pltpu.SemaphoreType.DMA((3,)),
-        pltpu.SemaphoreType.DMA((3,)),
+        pltpu.SemaphoreType.DMA((segments + 2,)),
+        pltpu.SemaphoreType.DMA((segments + 2,)),
         pltpu.SemaphoreType.DMA((segments, dates - 1)),
         pltpu.SemaphoreType.DMA((segments, dates - 1)),
         pltpu.SemaphoreType.DMA((dates - 1,)),
@@ -537,7 +551,7 @@
     ]
     anywhere = pl.BlockSpec(memory_space=pl.ANY)
     looks = pl.pallas_call(
-        functools.partial(fused_kernel, dates, lags, segments),
+        functools.partial(fused_kernel, dates, lags),
         out_shape=jax.ShapeDtypeStruct((2, LAGS, lines // LOOK_AZ, TILE), jnp.float32),
         in_specs=[anywhere] * 4,
         out_specs=pl.BlockSpec(memory_space=pltpu.VMEM),

time: 24 us -> 23.7 us (0.987)
  Pallas kernels: 22.4 us -> 22 us
    pallas_call x1, Pallas kernels: 22.4 us -> 22 us  [fused(): pl.pallas_call(functools.partial(fused_kernel, dates, lags), out_shape=ja...]
where the time goes in v3:
time: 23.7 us; the launch traced here: 23.5 us
  Pallas kernels  22 us (93%)
  local copies, waits for them, and re-layouts  1.47 us (6%)
    pallas_call x1, Pallas kernels, fused(): pl.pallas_call(functools.partial(fused_kernel, dates, lags), out_shape=ja...  22 us
    unnamed x1, local copies, waits for them, and re-layouts  1.47 us

profile of v3, /device:TPU:0, one launch (start us, length us, event | category | flops | bytes accessed | tf_op | source)
XLA Modules:
  0.0 23.5 jit_solution(4106859363660332923)
XLA Ops:
  0.0 22.0 %shard_map.46 = f32[2,8,8,128]{3,2,1,0:T(8,128)} custom-call(s32[1,2]{1,0:T(1,128)} %offset_hbm.1, s32[1,2]{1,0:T(1,128)} %index_hbm.1, f32[4]{0:T(128)} %shift_hbm.1, bf16[2,32,2560]{2,1,0:T(8,128)(2,1)} %bitcast.4), custom_call_target="tpu_custom_call" | custom-call | tf_op jit(solution)/shard_map/pallas_call | solution.py:553
  22.1 1.5 %copy.7 = f32[2,1,8,8,128]{4,3,2,1,0:T(8,128)} copy(f32[2,1,8,8,128]{4,3,2,1,0:T(8,128)} %bitcast.5) | data formatting | bytes 131072
